TPU v7x, 128 devices: a whole 4x4x4 slice. The times are simulated.
128 devices in a mesh: heads: 8 (over z, core), width: 4 (over y), sae: 4 (over x).
Axes of the slice: x: 4, y: 4, z: 4, core: 2. Of those that a mesh axis runs over, the one named last changes fastest.
Arguments:
- x_in: bfloat16 [512, 4608], P(None, 'width'), may hold values from -64 to 64
- doc_lengths: int32 [4], replicated, may hold values from 1 to 256, 512 in all
- attn_gain: float32 [4608], P('width'), may hold values from 0.25 to 1.75
- w_query: bfloat16 [4608, 4096], P('width', 'heads'), may hold values from -0.09375 to 0.09375
- w_key: bfloat16 [4608, 2048], P('width', 'heads'), may hold values from -0.09375 to 0.09375
- w_value: bfloat16 [4608, 2048], P('width', 'heads'), may hold values from -0.09375 to 0.09375
- w_out: bfloat16 [4096, 4608], P('heads', 'width'), may hold values from -0.09375 to 0.09375
- post_gain: float32 [4608], replicated, may hold values from 0.25 to 1.75
- enc_weight: bfloat16 [4608, 65536], P(None, ('heads', 'width', 'sae')), may hold values from -0.09375 to 0.09375
- enc_bias: float32 [65536], P(('heads', 'width', 'sae')), may hold values from -1.5 to 0.5
- dec_weight: bfloat16 [65536, 4608], P(('heads', 'width', 'sae')), may hold values from -1 to 1
- dec_bias: float32 [4608], replicated, may hold values from -5 to 5
Outputs:
- grad_enc: bfloat16 [4608, 65536], P(None, ('heads', 'width', 'sae'))
- grad_dec: bfloat16 [65536, 4608], P(('heads', 'width', 'sae'))
- total_loss: float32 [], replicated
Inputs may be any that keep to these rules, and one draw needn't show every extreme that they name: `doc_lengths`: lengths of the 4 documents packed in order; they sum to 512.
All inputs are finite; a program needn't handle non-finite values.
Results may differ from a plain program's by a relative error of at most 0.02.
Values may be sent and summed in bfloat16 or wider, within the bound.
A program may use at most 128 MiB of HBM per device.

v0:
```python
import jax
import jax.numpy as jnp
from jax import lax
from jax.sharding import PartitionSpec as P

D = 4608
HEADS = 32
HEAD_DIM = 128
norm_eps = 1e-06
soft_cap = 50.0
rope_base = 10000.0
l1_weight = 3.0


def rotary(values, position):
    half_dim = values.shape[-1] // 2
    frequency = rope_base ** (-2.0 * jnp.arange(half_dim, dtype=jnp.float32) / values.shape[-1])
    angles = position.astype(jnp.float32)[:, None] * frequency[None, :]
    cosine_table = jnp.cos(angles)[:, None, :]
    sine_table = jnp.sin(angles)[:, None, :]
    first_half = values[..., :half_dim]
    second_half = values[..., half_dim:]
    return jnp.concatenate(
        [
            first_half * cosine_table - second_half * sine_table,
            second_half * cosine_table + first_half * sine_table,
        ],
        axis=-1,
    )


def attend_rows(query_rows, key_rows, value_rows, allowed_rows, scale):
    scores = (
        jnp.einsum("tkgd,skd->kgts", query_rows, key_rows, preferred_element_type=jnp.float32)
        * scale
    )
    capped = soft_cap * jnp.tanh(scores / soft_cap)
    weights = jnp.where(allowed_rows[None, None], jnp.exp(capped), 0.0)
    totals = jnp.sum(weights, axis=-1, keepdims=True)
    probs_bf = (weights / totals).astype(jnp.bfloat16)
    return jnp.einsum(
        "kgts,skd->tkgd", probs_bf, value_rows, preferred_element_type=jnp.float32
    ).astype(jnp.bfloat16)


def per_device(
    x_in,
    doc_lengths,
    attn_gain,
    w_query,
    w_key,
    w_value,
    w_out,
    post_gain,
    enc_weight,
    enc_bias,
    dec_weight,
    dec_bias,
):
    tokens = x_in.shape[0]
    query_heads = w_query.shape[1] // HEAD_DIM
    value_heads = w_key.shape[1] // HEAD_DIM
    boundary = jnp.cumsum(doc_lengths)
    position = jnp.arange(tokens, dtype=jnp.int32)
    segment = jnp.sum((boundary[None, :] <= position[:, None]).astype(jnp.int32), axis=1)
    allowed = (segment[:, None] == segment[None, :]) & (position[None, :] <= position[:, None])
    x_float = x_in.astype(jnp.float32)
    scaled = (x_float * attn_gain).astype(jnp.bfloat16)
    query_part = jnp.dot(scaled, w_query, preferred_element_type=jnp.float32)
    key_part = jnp.dot(scaled, w_key, preferred_element_type=jnp.float32)
    value_part = jnp.dot(scaled, w_value, preferred_element_type=jnp.float32)
    square_part = jnp.sum(x_float * x_float, axis=1)
    query_raw, key_raw, value_raw, square_sums = lax.psum(
        (query_part, key_part, value_part, square_part), "width"
    )
    inverse_rms = lax.rsqrt(square_sums / D + norm_eps)
    query = rotary(
        (query_raw * inverse_rms[:, None]).reshape(tokens, query_heads, HEAD_DIM), position
    ).astype(jnp.bfloat16)
    key_rows = rotary(
        (key_raw * inverse_rms[:, None]).reshape(tokens, value_heads, HEAD_DIM), position
    ).astype(jnp.bfloat16)
    value_rows = (
        (value_raw * inverse_rms[:, None])
        .reshape(tokens, value_heads, HEAD_DIM)
        .astype(jnp.bfloat16)
    )
    query4 = query.reshape(tokens, value_heads, query_heads // value_heads, HEAD_DIM)
    pieces_out = attend_rows(query4, key_rows, value_rows, allowed, (D // HEADS) ** (-0.5))
    mixed = pieces_out.reshape(tokens, query_heads * HEAD_DIM)
    proj_part = jnp.dot(mixed, w_out, preferred_element_type=jnp.float32)
    attn_sum = lax.psum(proj_part, "heads")
    attn_local = attn_sum.astype(jnp.bfloat16)
    attn_proj, x_full = (
        lax.all_gather(attn_local, "width", axis=1, tiled=True),
        lax.all_gather(x_in, "width", axis=1, tiled=True),
    )
    proj_float = attn_proj.astype(jnp.float32)
    inverse_post = lax.rsqrt(jnp.sum(proj_float * proj_float, axis=1) / D + norm_eps)
    resid = (x_full.astype(jnp.float32) + proj_float * inverse_post[:, None] * post_gain).astype(
        jnp.bfloat16
    )
    centered = (resid.astype(jnp.float32) - dec_bias).astype(jnp.bfloat16)
    pre_acts = jnp.dot(centered, enc_weight, preferred_element_type=jnp.float32) + enc_bias
    latent_acts = jnp.maximum(pre_acts, 0.0).astype(jnp.bfloat16)
    row_norms = jnp.sqrt(jnp.sum(jnp.square(dec_weight.astype(jnp.float32)), axis=1) + norm_eps)
    act_sums = jnp.sum(latent_acts.astype(jnp.float32), axis=0)
    penalty_part = jnp.sum(act_sums * row_norms)
    recon_part = jnp.dot(latent_acts, dec_weight, preferred_element_type=jnp.float32)
    recon = lax.psum(recon_part, ("heads", "width", "sae")) + dec_bias
    error = recon - resid.astype(jnp.float32)
    squares_total = jnp.sum(error * error)
    penalty_total = lax.psum(penalty_part, ("heads", "width", "sae"))
    grad_recon = (2.0 / tokens * error).astype(jnp.bfloat16)
    total_loss = (squares_total + l1_weight * penalty_total) / (tokens * D)
    upstream = lax.dot_general(
        grad_recon, dec_weight, (((1,), (1,)), ((), ())), preferred_element_type=jnp.float32
    )
    grad_pre = jnp.where(pre_acts > 0, upstream + l1_weight * row_norms / tokens, 0.0).astype(
        jnp.bfloat16
    )
    grad_enc = lax.dot_general(
        centered, grad_pre, (((0,), (0,)), ((), ())), preferred_element_type=jnp.float32
    ).astype(jnp.bfloat16)
    decoder_term = lax.dot_general(
        latent_acts, grad_recon, (((0,), (0,)), ((), ())), preferred_element_type=jnp.float32
    )
    grad_dec = (
        decoder_term
        + l1_weight
        / tokens
        * act_sums[:, None]
        * dec_weight.astype(jnp.float32)
        / row_norms[:, None]
    ).astype(jnp.bfloat16)
    return (grad_enc, grad_dec, total_loss)


def solution(mesh):
    placed = (
        P(None, "width"),
        P(),
        P("width"),
        P("width", "heads"),
        P("width", "heads"),
        P("width", "heads"),
        P("heads", "width"),
        P(),
        P(None, ("heads", "width", "sae")),
        P(("heads", "width", "sae")),
        P(("heads", "width", "sae"), None),
        P(),
    )
    return jax.shard_map(
        per_device,
        mesh=mesh,
        in_specs=placed,
        out_specs=(P(None, ("heads", "width", "sae")), P(("heads", "width", "sae"), None), P()),
        check_vma=False,
    )
```

profile of v0, /device:TPU:1, one launch (start us, length us, event | category | flops | bytes accessed | tf_op | source)
XLA Modules:
  0.0 471.6 jit_solution(9375944868353371698)
XLA Ops:
  7.2 0.0 copy-start
  7.2 0.0 copy-start.3
  7.2 0.0 copy-start.11
  7.2 0.0 copy-start.10
  7.2 0.0 copy-start.13
  7.2 0.0 all-reduce.7.cloned.1.call-start
  7.3 3.6 fusion.23
  10.9 2.7 fusion.25
  13.6 0.0 copy-done.3
  13.6 0.0 copy-done.11
  13.6 1.3 fusion.27
  14.9 0.0 all-reduce.7.cloned.1.call-update
  15.0 0.0 all-gather.5.cloned.1.call-start
  15.0 0.2 reduce-window.8
  15.2 0.3 fusion.14
  15.5 9.5 %psum.50 = f32[512]{0:T(512)S(1)} all-reduce(f32[512]{0:T(512)S(1)} %fusion.14), channel_id=1, replica_groups=mesh['heads'=8,'width'=4,'sae'=4] {'width'}, use_global_device_ids=true, to_apply=%region_2.3 | all-reduce | flops 512 | bytes 4096 | tf_op jit(solution)/shard_map/psum | solution.py:73
  25.1 0.1 convert_reduce_fusion.1
  25.2 0.9 fusion.22
  26.1 1.7 multiply_cosine_fusion
  27.8 49.0 %all-reduce.7.cloned.1.call-done = (f32[512,256]{1,0:T(8,128)}, f32[512,512]{1,0:T(8,128)}, f32[512,256]{1,0:T(8,128)}) async-done(((f32[512,256]{1,0:T(8,128)}, f32[512,512]{1,0:T(8,128)}, f32[512,256]{1,0:T(8,128)}), (f32[512,256]{1,0:T(8,128)}, f32[512,512]{1,0:T(8,128)}, f32[512,256]{1,0:T(8,128)})) %all-reduce.7.cloned.1.call-update) | async-done | bytes 2097168 | tf_op jit(solution)/shard_map/psum | solution.py:73
  76.9 2.1 broadcast_multiply_fusion.1
  78.9 0.3 reshape.168
  79.2 1.5 fusion.40
  80.7 1.4 broadcast_multiply_fusion
  82.1 0.4 reshape.169
  82.4 0.0 copy-start.6
  82.4 0.0 copy-start.5
  82.5 1.8 subtract_convert_fusion
  84.3 0.1 copy.23
  84.3 0.1 copy.24
  84.4 0.1 copy.30
  84.6 0.0 copy-done.5
  84.6 1.3 subtract_convert_fusion.1
  85.9 0.0 copy-start.7
  85.9 2.9 fusion.12
  88.8 1.6 fusion.21
  90.4 0.9 fusion.41
  91.3 0.0 copy-start.8
  91.3 52.5 %all-reduce.8 = bf16[512,1152]{1,0:T(8,128)(2,1)} all-reduce(f32[512,1152]{1,0:T(8,128)S(1)} %fusion.41), channel_id=1, replica_groups=mesh['heads'=8,'width'=4,'sae'=4] {'heads'}, use_global_device_ids=true, to_apply=%region_8.9 | all-reduce | flops 589824 | bytes 3538944 | tf_op jit(solution)/shard_map/psum | solution.py:92
  143.8 0.0 all-gather.5.cloned.1.call-update
  143.8 0.0 all-gather.3.cloned.1.call-start
  143.8 0.7 all-gather.3.cloned.1.call-update
  144.5 0.2 all-reduce.5.cloned.1.call-start
  144.8 51.8 %all-gather.5.cloned.1.call-done = bf16[512,4608]{1,0:T(8,128)(2,1)} async-done(((bf16[512,1152]{1,0:T(8,128)(2,1)}), bf16[512,4608]{1,0:T(8,128)(2,1)}) %all-gather.5.cloned.1.call-update) | async-done | bytes 4718608 | tf_op jit(solution)/shard_map/all_gather | solution.py:95
  196.6 3.3 fusion
  199.9 0.0 copy-start.12
  200.0 51.3 %all-gather.3.cloned.1.call-done = bf16[512,4608]{1,0:T(8,128)(2,1)} async-done(((bf16[512,1152]{1,0:T(8,128)(2,1)}), bf16[512,4608]{1,0:T(8,128)(2,1)}) %all-gather.3.cloned.1.call-update) | async-done | bytes 4718608 | tf_op jit(solution)/shard_map/all_gather | solution.py:96
  251.3 0.0 copy-done.8
  251.3 5.9 %fusion.3 = bf16[512,4608]{1,0:T(8,128)(2,1)S(1)} fusion(bf16[512,4608]{1,0:T(8,128)(2,1)} %all-gather.5.cloned.1.call-done, bf16[512,4608]{1,0:T(8,128)(2,1)} %all-gather.3.cloned.1.call-done, f32[4608]{0:T(1024)S(1)} %copy-done.8, f32[512]{0:T(512)S(1)} %add_rsqrt_fusion), kind=kLoop, calls=%fused_computation.9 | loop fusion | flops 14155776 | bytes 14176256 | tf_op jit(solution)/shard_map/convert_element_type | solution.py:100
  257.2 0.0 copy-start.2
  257.2 0.0 slice-start.1
  257.3 6.4 %convert_reduce_fusion = (f32[512]{0:T(512)S(1)}, f32[512,512]{1,0:T(8,128)S(1)}) fusion(f32[512]{0:T(512)S(1)} %copy-done.12, bf16[4608,512]{1,0:T(8,128)(2,1)} %param.20, bf16[512,4608]{1,0:T(8,128)(2,1)S(1)} %fusion.3, f32[4608]{0:T(1024)S(1)} %copy-done.9), kind=kOutput, calls=%fused_computation.32 | convolution fusion | flops 2424045056 | bytes 10508288 | tf_op jit(solution)/shard_map/dot_general | solution.py:104
  263.7 5.1 %fusion.39 = f32[512,4608]{1,0:T(8,128)} fusion(bf16[512,4608]{1,0:T(8,128)(2,1)S(1)} %bitcast.41, f32[512,512]{1,0:T(8,128)S(1)} %get-tuple-element.25), kind=kOutput, calls=%fused_computation.69 | convolution fusion | flops 2416443392 | bytes 15204352 | tf_op jit(solution)/shard_map/dot_general | solution.py:109
  268.8 0.0 all-reduce.5.cloned.1.call-update
  268.8 3.3 fusion.5
  272.2 0.6 multiply_reduce_fusion.1
  272.8 65.8 %psum.55 = f32[]{:T(128)} all-reduce(f32[]{:T(128)} %get-tuple-element.16), channel_id=1, replica_groups=mesh['heads'=8,'width'=4,'sae'=4] {'heads','width','sae'}, use_global_device_ids=true, to_apply=%region_15.16 | all-reduce | flops 1 | bytes 8 | tf_op jit(solution)/shard_map/psum | solution.py:113
  339.2 94.4 %all-reduce.5.cloned.1.call-done = f32[512,4608]{1,0:T(8,128)} async-done(((f32[512,4608]{1,0:T(8,128)}), f32[512,4608]{1,0:T(8,128)}) %all-reduce.5.cloned.1.call-update) | async-done | bytes 9437200 | tf_op jit(solution)/shard_map/psum | solution.py:110
  433.6 8.4 %multiply_reduce_fusion = (f32[]{:T(128)}, bf16[512,4608]{1,0:T(8,128)(2,1)S(1)}) fusion(bf16[512,4608]{1,0:T(8,128)(2,1)} %copy-done.2, f32[512,4608]{1,0:T(8,128)} %all-reduce.5.cloned.1.call-done, f32[4608]{0:T(1024)S(1)} %copy-done.9), kind=kLoop, calls=%fused_computation.15 | loop fusion | flops 16515071 | bytes 18892804 | tf_op jit(solution)/shard_map/reduce_sum | solution.py:112
  442.0 6.7 %fusion.20 = bf16[512,512]{1,0:T(8,128)(2,1)S(1)} fusion(bf16[512,4608]{1,0:T(8,128)(2,1)S(1)} %get-tuple-element.7, bf16[512,4608]{1,0:T(8,128)(2,1)} %param.22, f32[512,512]{1,0:T(8,128)S(1)} %get-tuple-element.25, f32[512]{0:T(512)S(1)} %get-tuple-element.17), kind=kOutput, calls=%fused_computation.30 | convolution fusion | flops 2416967680 | bytes 11012096 | tf_op jit(solution)/shard_map/dot_general | solution.py:116
  448.7 6.8 %convolution_convert_fusion = bf16[4608,512]{1,0:T(8,128)(2,1)} fusion(bf16[512,512]{1,0:T(8,128)(2,1)S(1)} %fusion.20, bf16[512,4608]{1,0:T(8,128)(2,1)} %copy-done.2, f32[4608]{0:T(1024)S(1)} %copy-done.9), kind=kOutput, calls=%fused_computation.17 | convolution fusion | flops 2425356288 | bytes 9979904 | tf_op jit(solution)/shard_map/dot_general | solution.py:122
  456.1 0.0 copy-start.1
  456.1 7.8 %fusion.8 = bf16[512,4608]{1,0:T(8,128)(2,1)} fusion(bf16[512,4608]{1,0:T(8,128)(2,1)} %param.22, bf16[512,4608]{1,0:T(8,128)(2,1)} %copy-done.4, f32[512]{0:T(512)S(1)} %get-tuple-element.18, f32[512]{0:T(512)S(1)} %get-tuple-element.19, f32[512,512]{1,0:T(8,128)S(1)} %get-tuple-element.25), kind=kOutput, calls=%fused_computation.14 | convolution fusion | flops 2428239872 | bytes 15208448 | tf_op jit(solution)/shard_map/dot_general | solution.py:125
  463.9 0.0 copy-done.1
  (19 shorter events, 0.1 us)
Async XLA Ops:
  7.2 83.3 %copy-start = (bf16[512,1152]{1,0:T(8,128)(2,1)S(1)}, bf16[512,1152]{1,0:T(8,128)(2,1)}, u32[]{:S(2)}) copy-start(bf16[512,1152]{1,0:T(8,128)(2,1)} %param.18) | copy-start | bytes 3538948
  7.2 6.5 %copy-start.3 = (bf16[512,1152]{1,0:T(8,128)(2,1)S(1)}, bf16[512,1152]{1,0:T(8,128)(2,1)}, u32[]{:S(2)}) copy-start(bf16[512,1152]{1,0:T(8,128)(2,1)} %param.12) | copy-start | bytes 3538948
  7.2 6.4 %copy-start.11 = (f32[1152]{0:T(1024)S(1)}, f32[1152]{0:T(1024)}, u32[]{:S(2)}) copy-start(f32[1152]{0:T(1024)} %param.14) | copy-start | bytes 13828
  7.2 6.4 %copy-start.10 = (bf16[1152,256]{1,0:T(8,128)(2,1)S(1)}, bf16[1152,256]{1,0:T(8,128)(2,1)}, u32[]{:S(2)}) copy-start(bf16[1152,256]{1,0:T(8,128)(2,1)} %param.17) | copy-start | bytes 1769476
  7.2 7.8 %copy-start.13 = (s32[4]{0:T(128)S(1)}, s32[4]{0:T(128)}, u32[]{:S(2)}) copy-start(s32[4]{0:T(128)} %param.13) | copy-start | bytes 52
  7.2 69.6 %all-reduce.7.cloned.1.call-start = ((), (), s32[]{:S(2)}) async-start(), calls=%async_computation.3 | async-start | bytes 4194304 | tf_op jit(solution)/shard_map/psum | solution.py:73
  15.0 181.6 %all-gather.5.cloned.1.call-start = ((), (), s32[]{:S(2)}) async-start(), calls=%async_computation.1 | async-start | bytes 5898240 | tf_op jit(solution)/shard_map/all_gather | solution.py:95
  82.4 2.0 copy-start.6
  82.4 2.1 copy-start.5
  85.9 2.9 copy-start.7
  91.3 160.0 %copy-start.8 = (f32[4608]{0:T(1024)S(1)}, f32[4608]{0:T(1024)}, u32[]{:S(2)}) copy-start(f32[4608]{0:T(1024)} %param.19) | copy-start | bytes 55300
  143.8 107.5 %all-gather.3.cloned.1.call-start = ((), (), s32[]{:S(2)}) async-start(), calls=%async_computation | async-start | bytes 5898240 | tf_op jit(solution)/shard_map/all_gather | solution.py:96
  144.5 289.1 %all-reduce.5.cloned.1.call-start = ((), (), s32[]{:S(2)}) async-start(), calls=%async_computation.2 | async-start | bytes 18874368 | tf_op jit(solution)/shard_map/psum | solution.py:110
  199.9 57.3 %copy-start.9 = (f32[4608]{0:T(1024)S(1)}, f32[4608]{0:T(1024)}, u32[]{:S(2)}) copy-start(f32[4608]{0:T(1024)} %param.23) | copy-start | bytes 55300
  199.9 57.3 %copy-start.12 = (f32[512]{0:T(512)S(1)}, f32[512]{0:T(512)}, u32[]{:S(2)}) copy-start(f32[512]{0:T(512)} %param.21) | copy-start | bytes 6148
  251.3 12.4 %slice-start = ((s8[4718592]{0:T(1024)(128)(4,1)}), s8[4194304]{0:T(1024)(128)(4,1)S(1)}, s32[]{:S(2)}) async-start(s8[4718592]{0:T(1024)(128)(4,1)} %bitcast.40), calls=%async_computation.4 | async-start | bytes 8388608
  257.2 6.4 %copy-start.2 = (bf16[512,4608]{1,0:T(8,128)(2,1)}, bf16[512,4608]{1,0:T(8,128)(2,1)S(1)}, u32[]{:S(2)}) copy-start(bf16[512,4608]{1,0:T(8,128)(2,1)S(1)} %fusion.3) | copy-start | bytes 14155780
  257.2 6.5 %slice-start.1 = ((s8[4718592]{0:T(1024)(128)(4,1)}), s8[524288]{0:T(1024)(128)(4,1)S(1)}, s32[]{:S(2)}) async-start(s8[4718592]{0:T(1024)(128)(4,1)} %bitcast.40), calls=%async_computation.5 | async-start | bytes 1048576
  442.0 6.7 %copy-start.4 = (bf16[512,4608]{1,0:T(8,128)(2,1)}, bf16[512,4608]{1,0:T(8,128)(2,1)S(1)}, u32[]{:S(2)}) copy-start(bf16[512,4608]{1,0:T(8,128)(2,1)S(1)} %get-tuple-element.7) | copy-start | bytes 14155780
  456.1 7.9 %copy-start.1 = (bf16[512,1152]{1,0:T(8,128)(2,1)S(1)}, bf16[512,1152]{1,0:T(8,128)(2,1)}, u32[]{:S(2)}) copy-start(bf16[512,1152]{1,0:T(8,128)(2,1)} %param.18) | copy-start | bytes 3538948
Sparse Core Ops, SparseCore 0:
  15.1 61.7 all-reduce.6
  143.9 52.6 all-gather.4
  198.3 52.9 all-gather.2
  268.9 164.6 all-reduce.4
where the time goes:
time: 472 us
  waiting for transfers between devices  247 us (52%)
  blocking collectives  128 us (27%)
  matrix products  45.7 us (10%)
  other arithmetic  31.4 us (7%)
  between operations  16.5 us (3%)
    psum x1, waiting for transfers between devices, per_device(): recon = lax.psum(recon_part, ('heads', 'width', 'sae')) + dec_bias  94.4 us
    psum x1, blocking collectives, per_device(): penalty_total = lax.psum(penalty_part, ('heads', 'width', 'sae'))  65.8 us
    psum x1, blocking collectives, per_device(): attn_sum = lax.psum(proj_part, 'heads')  52.5 us
    all_gather x1, waiting for transfers between devices, per_device(): lax.all_gather(attn_local, 'width', axis=1, tiled=True)  51.8 us
    all_gather x1, waiting for transfers between devices, per_device(): lax.all_gather(x_in, 'width', axis=1, tiled=True)  51.3 us
    psum x1, waiting for transfers between devices, per_device(): lax.psum((query_part, key_part, value_part, square_part), 'width')  49 us
    psum x1, blocking collectives, per_device(): lax.psum((query_part, key_part, value_part, square_part), 'width')  9.54 us
  transfers between devices with their start and end apart: 4, of which 4 were waited for; matrix products, arithmetic and copies ran while one was open for 2% of the time, Pallas kernels for 0%

commit v1 on v0

--- a/solution.py
+++ b/solution.py
@@ -107,7 +107,7 @@
     act_sums = jnp.sum(latent_acts.astype(jnp.float32), axis=0)
     penalty_part = jnp.sum(act_sums * row_norms)
     recon_part = jnp.dot(latent_acts, dec_weight, preferred_element_type=jnp.float32)
-    recon = lax.psum(recon_part, ("heads", "width", "sae")) + dec_bias
+    recon = lax.psum(lax.psum(recon_part, "heads"), ("width", "sae")) + dec_bias
     error = recon - resid.astype(jnp.float32)
     squares_total = jnp.sum(error * error)
     penalty_total = lax.psum(penalty_part, ("heads", "width", "sae"))

time: 472 us -> 576 us (1.22)
  waiting for transfers between devices: 247 us -> 349 us
    psum x1 -> x2, waiting for transfers between devices: 94.4 us -> 196 us  [per_device(): recon = lax.psum(lax.psum(recon_part, 'heads'), ('width', 'sae')) + dec_bias]
  transfers between devices with their start and end apart: 4 -> 5, of which waited for: 4 -> 5; matrix products, arithmetic and copies ran while one was open for 2% -> 2% of each run, Pallas kernels for 0% -> 0%
where the time goes in v1:
time: 576 us; the launch traced here: 575 us
  waiting for transfers between devices  349 us (61%)
  blocking collectives  130 us (23%)
  matrix products  45.7 us (8%)
  other arithmetic  31.4 us (5%)
  between operations  16.5 us (3%)
    psum x2, waiting for transfers between devices, per_device(): recon = lax.psum(lax.psum(recon_part, 'heads'), ('width', 'sae')) + dec_bias  196 us
    psum x1, blocking collectives, per_device(): penalty_total = lax.psum(penalty_part, ('heads', 'width', 'sae'))  68.1 us
    psum x1, blocking collectives, per_device(): attn_sum = lax.psum(proj_part, 'heads')  52.5 us
    all_gather x1, waiting for transfers between devices, per_device(): lax.all_gather(attn_local, 'width', axis=1, tiled=True)  51.8 us
    all_gather x1, waiting for transfers between devices, per_device(): lax.all_gather(x_in, 'width', axis=1, tiled=True)  51.3 us
    psum x1, waiting for transfers between devices, per_device(): lax.psum((query_part, key_part, value_part, square_part), 'width')  49 us
  transfers between devices with their start and end apart: 5, of which 5 were waited for; matrix products, arithmetic and copies ran while one was open for 2% of the time, Pallas kernels for 0%

profile of v1, /device:TPU:1, one launch (start us, length us, event | category | flops | bytes accessed | tf_op | source)
XLA Modules:
  0.0 575.3 jit_solution(15833149714313977171)
XLA Ops:
  7.2 0.0 copy-start
  7.2 0.0 copy-start.3
  7.2 0.0 copy-start.11
  7.2 0.0 copy-start.10
  7.2 0.0 copy-start.13
  7.2 0.0 all-reduce.10.cloned.1.call-start
  7.3 3.6 fusion.23
  10.9 2.7 fusion.25
  13.6 0.0 copy-done.11
  13.6 1.3 fusion.27
  14.9 0.0 all-reduce.10.cloned.1.call-update
  15.0 0.0 all-gather.5.cloned.1.call-start
  15.0 0.2 reduce-window.8
  15.2 0.3 fusion.14
  15.5 9.5 %psum.57 = f32[512]{0:T(512)S(1)} all-reduce(f32[512]{0:T(512)S(1)} %fusion.14), channel_id=1, replica_groups=mesh['heads'=8,'width'=4,'sae'=4] {'width'}, use_global_device_ids=true, to_apply=%region_2.3 | all-reduce | flops 512 | bytes 4096 | tf_op jit(solution)/shard_map/psum | solution.py:73
  25.1 0.1 convert_reduce_fusion.1
  25.2 0.9 fusion.22
  26.1 1.7 multiply_cosine_fusion
  27.8 49.0 %all-reduce.10.cloned.1.call-done = (f32[512,256]{1,0:T(8,128)}, f32[512,512]{1,0:T(8,128)}, f32[512,256]{1,0:T(8,128)}) async-done(((f32[512,256]{1,0:T(8,128)}, f32[512,512]{1,0:T(8,128)}, f32[512,256]{1,0:T(8,128)}), (f32[512,256]{1,0:T(8,128)}, f32[512,512]{1,0:T(8,128)}, f32[512,256]{1,0:T(8,128)})) %all-reduce.10.cloned.1.call-update) | async-done | bytes 2097168 | tf_op jit(solution)/shard_map/psum | solution.py:73
  76.9 2.1 broadcast_multiply_fusion.1
  78.9 0.3 reshape.168
  79.2 1.5 fusion.40
  80.7 1.4 broadcast_multiply_fusion
  82.1 0.4 reshape.169
  82.4 0.0 copy-start.6
  82.4 0.0 copy-start.5
  82.5 1.8 subtract_convert_fusion
  84.3 0.1 copy.23
  84.3 0.1 copy.24
  84.4 0.1 copy.30
  84.6 0.0 copy-done.5
  84.6 1.4 subtract_convert_fusion.1
  86.0 0.0 copy-start.7
  86.0 2.9 fusion.12
  88.9 1.6 fusion.21
  90.5 0.9 fusion.41
  91.3 0.0 copy-start.8
  91.3 52.5 %all-reduce.11 = bf16[512,1152]{1,0:T(8,128)(2,1)} all-reduce(f32[512,1152]{1,0:T(8,128)S(1)} %fusion.41), channel_id=1, replica_groups=mesh['heads'=8,'width'=4,'sae'=4] {'heads'}, use_global_device_ids=true, to_apply=%region_8.9 | all-reduce | flops 589824 | bytes 3538944 | tf_op jit(solution)/shard_map/psum | solution.py:92
  143.8 0.0 all-gather.5.cloned.1.call-update
  143.8 0.0 all-gather.3.cloned.1.call-start
  143.9 0.7 all-gather.3.cloned.1.call-update
  144.6 0.2 all-reduce.6.cloned.1.call-start
  144.8 51.8 %all-gather.5.cloned.1.call-done = bf16[512,4608]{1,0:T(8,128)(2,1)} async-done(((bf16[512,1152]{1,0:T(8,128)(2,1)}), bf16[512,4608]{1,0:T(8,128)(2,1)}) %all-gather.5.cloned.1.call-update) | async-done | bytes 4718608 | tf_op jit(solution)/shard_map/all_gather | solution.py:95
  196.6 3.3 fusion
  200.0 0.0 copy-start.12
  200.0 51.3 %all-gather.3.cloned.1.call-done = bf16[512,4608]{1,0:T(8,128)(2,1)} async-done(((bf16[512,1152]{1,0:T(8,128)(2,1)}), bf16[512,4608]{1,0:T(8,128)(2,1)}) %all-gather.3.cloned.1.call-update) | async-done | bytes 4718608 | tf_op jit(solution)/shard_map/all_gather | solution.py:96
  251.3 5.9 %fusion.3 = bf16[512,4608]{1,0:T(8,128)(2,1)S(1)} fusion(bf16[512,4608]{1,0:T(8,128)(2,1)} %all-gather.5.cloned.1.call-done, bf16[512,4608]{1,0:T(8,128)(2,1)} %all-gather.3.cloned.1.call-done, f32[4608]{0:T(1024)S(1)} %copy-done.8, f32[512]{0:T(512)S(1)} %add_rsqrt_fusion), kind=kLoop, calls=%fused_computation.9 | loop fusion | flops 14155776 | bytes 14176256 | tf_op jit(solution)/shard_map/convert_element_type | solution.py:100
  257.3 0.0 copy-start.2
  257.3 0.0 slice-start.1
  257.3 6.4 %convert_reduce_fusion = (f32[512]{0:T(512)S(1)}, f32[512,512]{1,0:T(8,128)S(1)}) fusion(f32[512]{0:T(512)S(1)} %copy-done.12, bf16[4608,512]{1,0:T(8,128)(2,1)} %param.20, bf16[512,4608]{1,0:T(8,128)(2,1)S(1)} %fusion.3, f32[4608]{0:T(1024)S(1)} %copy-done.9), kind=kOutput, calls=%fused_computation.32 | convolution fusion | flops 2424045056 | bytes 10508288 | tf_op jit(solution)/shard_map/dot_general | solution.py:104
  263.7 5.1 fusion.39
  268.8 0.0 all-reduce.6.cloned.1.call-update
  268.8 0.0 all-reduce.8.cloned.1.call-start
  268.9 114.4 %all-reduce.6.cloned.1.call-done = f32[512,4608]{1,0:T(8,128)} async-done(((f32[512,4608]{1,0:T(8,128)}), f32[512,4608]{1,0:T(8,128)}) %all-reduce.6.cloned.1.call-update) | async-done | bytes 9437200 | tf_op jit(solution)/shard_map/psum | solution.py:110
  383.3 0.0 all-reduce.8.cloned.1.call-update
  383.3 3.3 fusion.5
  386.6 0.6 multiply_reduce_fusion.1
  387.3 68.1 %psum.63 = f32[]{:T(128)} all-reduce(f32[]{:T(128)} %get-tuple-element.16), channel_id=1, replica_groups=mesh['heads'=8,'width'=4,'sae'=4] {'heads','width','sae'}, use_global_device_ids=true, to_apply=%region_16.17 | all-reduce | flops 1 | bytes 8 | tf_op jit(solution)/shard_map/psum | solution.py:113
  456.0 81.3 %all-reduce.8.cloned.1.call-done = f32[512,4608]{1,0:T(8,128)} async-done(((f32[512,4608]{1,0:T(8,128)}), f32[512,4608]{1,0:T(8,128)}) %all-reduce.8.cloned.1.call-update) | async-done | bytes 9437200 | tf_op jit(solution)/shard_map/psum | solution.py:110
  537.3 8.4 %multiply_reduce_fusion = (f32[]{:T(128)}, bf16[512,4608]{1,0:T(8,128)(2,1)S(1)}) fusion(bf16[512,4608]{1,0:T(8,128)(2,1)} %copy-done.2, f32[512,4608]{1,0:T(8,128)} %all-reduce.8.cloned.1.call-done, f32[4608]{0:T(1024)S(1)} %copy-done.9), kind=kLoop, calls=%fused_computation.15 | loop fusion | flops 16515071 | bytes 18892804 | tf_op jit(solution)/shard_map/reduce_sum | solution.py:112
  545.6 6.7 %fusion.20 = bf16[512,512]{1,0:T(8,128)(2,1)S(1)} fusion(bf16[512,4608]{1,0:T(8,128)(2,1)S(1)} %get-tuple-element.7, bf16[512,4608]{1,0:T(8,128)(2,1)} %param.22, f32[512,512]{1,0:T(8,128)S(1)} %get-tuple-element.25, f32[512]{0:T(512)S(1)} %get-tuple-element.17), kind=kOutput, calls=%fused_computation.30 | convolution fusion | flops 2416967680 | bytes 11012096 | tf_op jit(solution)/shard_map/dot_general | solution.py:116
  552.3 6.7 %convolution_convert_fusion = bf16[4608,512]{1,0:T(8,128)(2,1)} fusion(bf16[512,512]{1,0:T(8,128)(2,1)S(1)} %fusion.20, bf16[512,4608]{1,0:T(8,128)(2,1)} %copy-done.2, f32[4608]{0:T(1024)S(1)} %copy-done.9), kind=kOutput, calls=%fused_computation.17 | convolution fusion | flops 2425356288 | bytes 9979904 | tf_op jit(solution)/shard_map/dot_general | solution.py:122
  559.7 0.0 copy-start.1
  559.7 7.8 %fusion.8 = bf16[512,4608]{1,0:T(8,128)(2,1)} fusion(bf16[512,4608]{1,0:T(8,128)(2,1)} %param.22, bf16[512,4608]{1,0:T(8,128)(2,1)} %copy-done.4, f32[512]{0:T(512)S(1)} %get-tuple-element.18, f32[512]{0:T(512)S(1)} %get-tuple-element.19, f32[512,512]{1,0:T(8,128)S(1)} %get-tuple-element.25), kind=kOutput, calls=%fused_computation.14 | convolution fusion | flops 2428239872 | bytes 15208448 | tf_op jit(solution)/shard_map/dot_general | solution.py:125
  (22 shorter events, 0.1 us)
Async XLA Ops:
  7.2 83.3 %copy-start = (bf16[512,1152]{1,0:T(8,128)(2,1)S(1)}, bf16[512,1152]{1,0:T(8,128)(2,1)}, u32[]{:S(2)}) copy-start(bf16[512,1152]{1,0:T(8,128)(2,1)} %param.18) | copy-start | bytes 3538948
  7.2 6.5 %copy-start.3 = (bf16[512,1152]{1,0:T(8,128)(2,1)S(1)}, bf16[512,1152]{1,0:T(8,128)(2,1)}, u32[]{:S(2)}) copy-start(bf16[512,1152]{1,0:T(8,128)(2,1)} %param.12) | copy-start | bytes 3538948
  7.2 6.4 %copy-start.11 = (f32[1152]{0:T(1024)S(1)}, f32[1152]{0:T(1024)}, u32[]{:S(2)}) copy-start(f32[1152]{0:T(1024)} %param.14) | copy-start | bytes 13828
  7.2 6.4 %copy-start.10 = (bf16[1152,256]{1,0:T(8,128)(2,1)S(1)}, bf16[1152,256]{1,0:T(8,128)(2,1)}, u32[]{:S(2)}) copy-start(bf16[1152,256]{1,0:T(8,128)(2,1)} %param.17) | copy-start | bytes 1769476
  7.2 7.8 %copy-start.13 = (s32[4]{0:T(128)S(1)}, s32[4]{0:T(128)}, u32[]{:S(2)}) copy-start(s32[4]{0:T(128)} %param.13) | copy-start | bytes 52
  7.2 69.6 %all-reduce.10.cloned.1.call-start = ((), (), s32[]{:S(2)}) async-start(), calls=%async_computation.4 | async-start | bytes 4194304 | tf_op jit(solution)/shard_map/psum | solution.py:73
  15.0 181.6 %all-gather.5.cloned.1.call-start = ((), (), s32[]{:S(2)}) async-start(), calls=%async_computation.1 | async-start | bytes 5898240 | tf_op jit(solution)/shard_map/all_gather | solution.py:95
  82.4 2.0 copy-start.6
  82.4 2.1 copy-start.5
  86.0 2.9 copy-start.7
  91.3 160.0 %copy-start.8 = (f32[4608]{0:T(1024)S(1)}, f32[4608]{0:T(1024)}, u32[]{:S(2)}) copy-start(f32[4608]{0:T(1024)} %param.19) | copy-start | bytes 55300
  143.8 107.5 %all-gather.3.cloned.1.call-start = ((), (), s32[]{:S(2)}) async-start(), calls=%async_computation | async-start | bytes 5898240 | tf_op jit(solution)/shard_map/all_gather | solution.py:96
  144.6 238.7 %all-reduce.6.cloned.1.call-start = ((), (), s32[]{:S(2)}) async-start(), calls=%async_computation.2 | async-start | bytes 18874368 | tf_op jit(solution)/shard_map/psum | solution.py:110
  200.0 57.3 %copy-start.9 = (f32[4608]{0:T(1024)S(1)}, f32[4608]{0:T(1024)}, u32[]{:S(2)}) copy-start(f32[4608]{0:T(1024)} %param.23) | copy-start | bytes 55300
  200.0 57.3 %copy-start.12 = (f32[512]{0:T(512)S(1)}, f32[512]{0:T(512)}, u32[]{:S(2)}) copy-start(f32[512]{0:T(512)} %param.21) | copy-start | bytes 6148
  251.3 12.4 %slice-start = ((s8[4718592]{0:T(1024)(128)(4,1)}), s8[4194304]{0:T(1024)(128)(4,1)S(1)}, s32[]{:S(2)}) async-start(s8[4718592]{0:T(1024)(128)(4,1)} %bitcast.40), calls=%async_computation.5 | async-start | bytes 8388608
  257.3 6.4 %copy-start.2 = (bf16[512,4608]{1,0:T(8,128)(2,1)}, bf16[512,4608]{1,0:T(8,128)(2,1)S(1)}, u32[]{:S(2)}) copy-start(bf16[512,4608]{1,0:T(8,128)(2,1)S(1)} %fusion.3) | copy-start | bytes 14155780
  257.3 6.4 %slice-start.1 = ((s8[4718592]{0:T(1024)(128)(4,1)}), s8[524288]{0:T(1024)(128)(4,1)S(1)}, s32[]{:S(2)}) async-start(s8[4718592]{0:T(1024)(128)(4,1)} %bitcast.40), calls=%async_computation.6 | async-start | bytes 1048576
  268.8 268.4 %all-reduce.8.cloned.1.call-start = ((), (), s32[]{:S(2)}) async-start(), calls=%async_computation.3 | async-start | bytes 18874368 | tf_op jit(solution)/shard_map/psum | solution.py:110
  545.6 6.7 %copy-start.4 = (bf16[512,4608]{1,0:T(8,128)(2,1)}, bf16[512,4608]{1,0:T(8,128)(2,1)S(1)}, u32[]{:S(2)}) copy-start(bf16[512,4608]{1,0:T(8,128)(2,1)S(1)} %get-tuple-element.7) | copy-start | bytes 14155780
  559.7 7.9 %copy-start.1 = (bf16[512,1152]{1,0:T(8,128)(2,1)S(1)}, bf16[512,1152]{1,0:T(8,128)(2,1)}, u32[]{:S(2)}) copy-start(bf16[512,1152]{1,0:T(8,128)(2,1)} %param.18) | copy-start | bytes 3538948
Sparse Core Ops, SparseCore 0:
  15.1 61.7 all-reduce.9
  144.0 52.6 all-gather.4
  198.3 52.9 all-gather.2
  269.0 114.2 all-reduce.5
  386.8 150.4 all-reduce.7
